TPU v7x, 256 devices: a whole 4x4x8 slice. The times are simulated.
256 devices in a mesh: seq: 32 (over y, z), grp: 8 (over x, core).
Axes of the slice: x: 4, y: 4, z: 8, core: 2. Of those that a mesh axis runs over, the one named last changes fastest.
Arguments:
- mixer_input: bfloat16 [5120, 32768], P('grp', 'seq'), may hold values from -5 to 5
- step_sizes: float32 [80, 32768], P('grp', 'seq'), may hold values from 0 to 1, as said below
- decay_rates: float32 [80], P('grp'), may hold values from 1 to 2
- skip_gain: float32 [80], P('grp'), may hold values from 0.5 to 1.5
- input_basis: bfloat16 [32768, 128], P('seq'), may hold values from -5 to 5
- output_basis: bfloat16 [32768, 128], P('seq'), may hold values from -0.5 to 0.5
- out_weight: bfloat16 [5120, 2560], P(None, 'grp'), may hold values from -0.078125 to 0.078125
Outputs:
- layer_output: bfloat16 [32768, 2560], P('seq', 'grp')
Inputs may be any that keep to these rules, and one draw needn't show every extreme that they name: `step_sizes`: positive step sizes.
All inputs are finite; a program needn't handle non-finite values.
Results may differ from a plain program's by a relative error of at most 0.0065.
Values may be sent and summed in bfloat16 or wider, within the bound.
A program may use at most 128 MiB of HBM per device.

v0:
```python
import jax
import jax.numpy as jnp
from jax import lax
from jax.sharding import PartitionSpec as P

HP = 64
N = 128
GROUP = 256


def carry_in(total_log, final_state):
    peers, here = (lax.axis_size("seq"), lax.axis_index("seq"))

    def shifted(value, d):
        return lax.ppermute(value, "seq", [(i, i + d) for i in range(peers - d)])

    decay = shifted(jnp.exp(total_log), 1)
    decay = jnp.where(here >= 1, decay, jnp.ones_like(decay))
    state = shifted(final_state, 1)
    d = 1
    while d < peers:
        decay_r, state_r = (shifted(decay, d), shifted(state, d))
        reached = here >= d
        state = jnp.where(reached, decay[:, None, None] * state_r + state, state)
        decay = jnp.where(reached, decay * decay_r, decay)
        d *= 2
    return state


def on_device(
    mixer_input, step_sizes, decay_rates, skip_gain, input_basis, output_basis, out_weight
):
    heads_here = step_sizes.shape[0]
    tokens_here = step_sizes.shape[1]
    count = tokens_here // GROUP
    channels = mixer_input.reshape(heads_here, HP, count, GROUP)
    log_decay = -(decay_rates[:, None] * step_sizes).reshape(heads_here, count, GROUP)
    steps_blocked = step_sizes.reshape(heads_here, count, GROUP)
    running = jnp.cumsum(log_decay, axis=2)
    basis_in_blocked = input_basis.reshape(count, GROUP, N)
    basis_out_blocked = output_basis.reshape(count, GROUP, N)
    gram = jnp.einsum(
        "cin,cjn->cij", basis_out_blocked, basis_in_blocked, preferred_element_type=jnp.float32
    )
    rows_index = lax.broadcasted_iota(jnp.int32, (GROUP, GROUP), 0)
    cols_index = lax.broadcasted_iota(jnp.int32, (GROUP, GROUP), 1)
    causal = rows_index >= cols_index
    gaps = running[:, :, :, None] - running[:, :, None, :]
    mixing = jnp.where(
        causal,
        gram[None] * jnp.exp(jnp.where(causal, gaps, 0.0)) * steps_blocked[:, :, None, :],
        0.0,
    ).astype(jnp.bfloat16)
    inner = jnp.einsum("hcij,hpcj->hpci", mixing, channels, preferred_element_type=jnp.float32)
    tail = jnp.exp(running[:, :, -1:] - running) * steps_blocked
    weighted_terms = (basis_in_blocked.astype(jnp.float32)[None] * tail[:, :, :, None]).astype(
        jnp.bfloat16
    )
    summaries = jnp.einsum(
        "hcjn,hpcj->chnp", weighted_terms, channels, preferred_element_type=jnp.float32
    )
    block_decay = jnp.exp(running[:, :, -1])

    def advance(state, pair):
        decay, digest_record = pair
        return (decay[:, None, None] * state + digest_record, state)

    zero_state = jnp.zeros((heads_here, N, HP), jnp.float32)
    final_state, entering = lax.scan(advance, zero_state, (block_decay.T, summaries))
    block_sums = jnp.sum(log_decay, axis=2)
    prefix = jnp.exp(jnp.cumsum(block_sums, axis=1) - block_sums)
    total_log = jnp.sum(block_sums, axis=1)
    basis_out_wide = basis_out_blocked.astype(jnp.float32)
    within = jnp.exp(running)[:, None]
    direct = skip_gain[:, None, None, None] * channels.astype(jnp.float32)
    carried = carry_in(total_log, final_state)
    states = entering + prefix.T[:, :, None, None] * carried[None]
    from_state = jnp.einsum(
        "cin,chnp->hpci", basis_out_wide, states, precision=lax.Precision.HIGHEST
    )
    mixed = inner + from_state * within + direct
    mixed_columns = mixed.astype(jnp.bfloat16).reshape(heads_here * HP, tokens_here)
    result = jnp.einsum(
        "kt,kd->td",
        lax.all_gather(mixed_columns, "grp", axis=0, tiled=True),
        out_weight,
        preferred_element_type=jnp.float32,
    )
    return result.astype(jnp.bfloat16)


def solution(mesh):
    placed = (
        P("grp", "seq"),
        P("grp", "seq"),
        P("grp"),
        P("grp"),
        P("seq", None),
        P("seq", None),
        P(None, "grp"),
    )
    return jax.shard_map(
        on_device, mesh=mesh, in_specs=placed, out_specs=P("seq", "grp"), check_vma=False
    )
```

profile of v0, /device:TPU:1, one launch (start us, length us, event | category | flops | bytes accessed | tf_op | source)
XLA Modules:
  0.0 231.2 jit_solution(14767401530149646596)
XLA Ops:
  6.5 1.0 mul.141
  7.6 1.0 fusion.19
  8.6 0.6 copy-done.5
  9.3 2.3 reduce-window.6
  11.6 0.2 slice_reduce_fusion
  11.8 0.1 broadcast_add_fusion
  12.0 0.1 slice.15
  12.1 0.1 copy.33
  12.2 0.1 copy.34
  12.3 0.6 fusion.20
  12.9 1.8 convert_element_type.24
  14.7 3.8 %reshape.94 = bf16[10,64,4,256]{3,2,1,0:T(4,128)(2,1)} reshape(bf16[640,1024]{1,0:T(8,128)(2,1)} %param.9) | data formatting | bytes 2621440 | tf_op jit(solution)/shard_map/reshape | solution.py:36
  18.5 5.6 %fusion.8 = f32[4,10,128,64]{3,2,1,0:T(8,128)} fusion(f32[10,4,256]{2,0,1:T(8,128)S(1)} %copy.35, f32[4,256,128]{2,1,0:T(8,128)} %convert_element_type.24, bf16[10,64,4,256]{3,2,1,0:T(4,128)(2,1)} %reshape.94), kind=kOutput, calls=%fused_computation.13 | convolution fusion | flops 170393600 | bytes 3186688 | tf_op jit(solution)/shard_map/hcjn,hpcj->chnp/dot_general | solution.py:59
  24.1 15.7 %while.13 = (s32[]{:T(128)}, f32[10,128,64]{2,1,0:T(8,128)}, f32[4,10,128,64]{3,2,1,0:T(8,128)}, f32[4,10]{1,0:T(4,128)S(1)}, f32[4,10,128,64]{3,2,1,0:T(8,128)}, /*index=5*/s32[]{:T(128)}, s32[]{:T(128)}) while((s32[]{:T(128)}, f32[10,128,64]{2,1,0:T(8,128)}, f32[4,10,128,64]{3,2,1,0:T(8,128)}, f32[4,10]{1,0:T(4,128)S(1)}, ...), condition=%wide.region_3.4_spmd.clone, body=%wide.region_2.3_spmd.clone.sunk | while | flops 327683 | bytes 2293988 | solution.py:69
  24.1 0.9 bitcast_dynamic-update-slice_fusion.2
  25.1 2.1 bitcast_add_fusion.2
  27.1 2.0 bitcast_dynamic-update-slice_fusion.2
  29.1 2.3 bitcast_add_fusion.2
  31.4 2.0 bitcast_dynamic-update-slice_fusion.2
  33.4 2.3 bitcast_add_fusion.2
  35.6 2.0 bitcast_dynamic-update-slice_fusion.2
  37.6 2.3 bitcast_add_fusion.2
  39.9 2.1 copy.39
  41.9 5.1 %collective-permute-start.5 = (f32[10,128,64]{1,2,0:T(8,128)}, f32[10,128,64]{1,2,0:T(8,128)}, u32[]{:S(2)}, u32[]{:S(2)}) collective-permute-start(f32[10,128,64]{1,2,0:T(8,128)} %copy.39), channel_id=1, source_target_pairs={{0,8},{8,16},{16,24},{24,32},{32,40},{40,48},{48,56},{56,64},{64,7... | collective-permute-start | bytes 983048 | tf_op jit(solution)/shard_map/ppermute | solution.py:15
  47.0 6.0 %collective-permute-done.5 = f32[10,128,64]{1,2,0:T(8,128)} collective-permute-done((f32[10,128,64]{1,2,0:T(8,128)}, f32[10,128,64]{1,2,0:T(8,128)}, u32[]{:S(2)}, u32[]{:S(2)}) %collective-permute-start.5) | collective-permute-done | bytes 327712 | tf_op jit(solution)/shard_map/ppermute | solution.py:15
  53.0 4.8 %collective-permute-start.6 = (f32[10,128,64]{1,2,0:T(8,128)}, f32[10,128,64]{1,2,0:T(8,128)}, u32[]{:S(2)}, u32[]{:S(2)}) collective-permute-start(f32[10,128,64]{1,2,0:T(8,128)} %collective-permute-done.5), channel_id=1, source_target_pairs={{0,8},{8,16},{16,24},{24,32},{32,40},{40,48},{48,56},{56,64},{64,7... | collective-permute-start | bytes 983048 | tf_op jit(solution)/shard_map/ppermute | solution.py:15
  57.8 2.8 %collective-permute-start = (f32[10]{0:T(128)S(1)}, f32[10]{0:T(128)S(1)}, u32[]{:S(2)}, u32[]{:S(2)}) collective-permute-start(f32[10]{0:T(128)S(1)} %negate_exponential_fusion), channel_id=1, source_target_pairs={{0,8},{8,16},{16,24},{24,32},{32,40},{40,48},{48,56},{56,64},{64,7... | collective-permute-start | bytes 128 | tf_op jit(solution)/shard_map/ppermute | solution.py:15
  60.7 2.2 collective-permute-done
  62.8 0.0 collective-permute-done.6
  62.9 1.9 add_select_fusion.4
  64.8 6.6 %collective-permute-start.7 = (f32[10,128,64]{1,2,0:T(8,128)}, f32[10,128,64]{1,2,0:T(8,128)}, u32[]{:S(2)}, u32[]{:S(2)}) collective-permute-start(f32[10,128,64]{1,2,0:T(8,128)} %add_select_fusion.4), channel_id=1, source_target_pairs={{0,16},{8,24},{16,32},{24,40},{32,48},{40,56},{48,64},{56,72},{64,... | collective-permute-start | bytes 983048 | tf_op jit(solution)/shard_map/ppermute | solution.py:15
  71.3 5.0 %collective-permute-start.1 = (f32[10]{0:T(128)S(1)}, f32[10]{0:T(128)S(1)}, u32[]{:S(2)}, u32[]{:S(2)}) collective-permute-start(f32[10]{0:T(128)S(1)} %broadcast_select_fusion.1), channel_id=1, source_target_pairs={{0,8},{8,16},{16,24},{24,32},{32,40},{40,48},{48,56},{56,64},{64,7... | collective-permute-start | bytes 128 | tf_op jit(solution)/shard_map/ppermute | solution.py:15
  76.3 0.7 collective-permute-done.1
  77.0 1.9 add_select_fusion.3
  79.0 20.3 %collective-permute-start.8 = (f32[10,128,64]{1,2,0:T(8,128)}, f32[10,128,64]{1,2,0:T(8,128)}, u32[]{:S(2)}, u32[]{:S(2)}) collective-permute-start(f32[10,128,64]{1,2,0:T(8,128)} %add_select_fusion.3), channel_id=1, source_target_pairs={{0,32},{8,40},{16,48},{24,56},{32,64},{40,72},{48,80},{56,88},{64,... | collective-permute-start | bytes 983048 | tf_op jit(solution)/shard_map/ppermute | solution.py:15
  99.3 2.2 fusion.22
  101.5 1.5 reshape.95
  103.0 0.9 reduce_sum.18
  103.9 0.8 reduce_window_sum.43
  104.7 1.3 collective-permute-start.2
  106.0 7.2 %collective-permute-done.2 = f32[10]{0:T(128)S(1)} collective-permute-done((f32[10]{0:T(128)}, f32[10]{0:T(128)S(1)}, u32[]{:S(2)}, u32[]{:S(2)}) %collective-permute-start.2) | collective-permute-done | bytes 72 | tf_op jit(solution)/shard_map/ppermute | solution.py:15
  113.1 0.7 broadcast_select_fusion.2
  113.8 1.9 add_select_fusion.2
  115.7 5.6 %collective-permute-start.9 = (f32[10,128,64]{1,2,0:T(8,128)}, f32[10,128,64]{1,2,0:T(8,128)}, u32[]{:S(2)}, u32[]{:S(2)}) collective-permute-start(f32[10,128,64]{1,2,0:T(8,128)} %add_select_fusion.2), channel_id=1, source_target_pairs={{0,64},{8,72},{16,80},{24,88},{32,96},{40,104},{48,112},{56,120},{... | collective-permute-start | bytes 983048 | tf_op jit(solution)/shard_map/ppermute | solution.py:15
  121.3 0.7 exponential_bitcast_fusion
  122.0 0.1 copy.38
  122.1 3.8 %collective-permute-start.3 = (f32[10]{0:T(128)}, f32[10]{0:T(128)S(1)}, u32[]{:S(2)}, u32[]{:S(2)}) collective-permute-start(f32[10]{0:T(128)} %copy-done.13), channel_id=1, source_target_pairs={{0,32},{8,40},{16,48},{24,56},{32,64},{40,72},{48,80},{56,88},{64,... | collective-permute-start | bytes 128 | tf_op jit(solution)/shard_map/ppermute | solution.py:15
  125.9 0.9 collective-permute-done.3
  126.8 0.7 broadcast_select_fusion.3
  127.5 1.2 add_select_fusion.1
  128.7 8.7 %collective-permute-start.10 = (f32[10,128,64]{1,2,0:T(8,128)S(1)}, f32[10,128,64]{1,2,0:T(8,128)S(1)}, u32[]{:S(2)}, u32[]{:S(2)}) collective-permute-start(f32[10,128,64]{1,2,0:T(8,128)S(1)} %add_select_fusion.1), channel_id=1, source_target_pairs={{0,128},{8,136},{16,144},{24,152},{32,160},{40,168},{48,176},{56,1... | collective-permute-start | bytes 983048 | tf_op jit(solution)/shard_map/ppermute | solution.py:15
  137.4 0.6 iota_compare_fusion
  138.0 1.3 collective-permute-start.4
  139.3 3.3 %collective-permute-done.4 = f32[10]{0:T(128)S(1)} collective-permute-done((f32[10]{0:T(128)S(1)}, f32[10]{0:T(128)S(1)}, u32[]{:S(2)}, u32[]{:S(2)}) %collective-permute-start.4) | collective-permute-done | bytes 72 | tf_op jit(solution)/shard_map/ppermute | solution.py:15
  142.6 0.8 add_select_fusion
  143.5 2.0 copy.40
  145.5 0.0 copy-start.14
  145.6 4.4 %fusion.12 = f32[4,10,64,256]{3,2,0,1:T(8,128)S(1)} fusion(bf16[4,256,128,1]{2,1,0,3:T(8,128)(2,1)S(1)} %bitcast.46, f32[4,10,128,64]{3,2,1,0:T(8,128)} %get-tuple-element.33, f32[10,128,64]{2,1,0:T(8,128)} %copy.40, f32[4,10]{1,0:T(4,128)S(1)} %copy.38), kind=kOutput, calls=%fused_computation.18 | convolution fusion | flops 1007288320 | bytes 4522144 | tf_op jit(solution)/shard_map/cin,chnp->hpci/dot_general | solution.py:78
  150.0 4.0 %fusion.11 = bf16[10,64,4,256]{3,1,2,0:T(8,128)(2,1)S(1)} fusion(f32[4,10,64,256]{3,2,0,1:T(8,128)S(1)} %fusion.12, f32[10,4,256]{2,1,0:T(4,128)S(1)} %copy-done.9, f32[10,4,256]{2,1,0:T(4,128)S(1)} %copy-done.7, f32[4,256,256]{2,1,0:T(8,128)S(1)} %copy-done.2, pred[256,256]{1,0:T(8,128)(4,1)S(1)} %copy-done.10, bf16[10,64,4,256]{3,2,1,0:T(4,128)(2,1)S(1)} %copy-done.1, ...), kind=kOutput, calls=%fused_computation.17 | convolution fusion | flops 355205120 | bytes 6479912 | tf_op jit(solution)/shard_map/hcij,hpcj->hpci/dot_general | solution.py:54
  154.0 1.0 copy.43
  155.0 1.4 copy.47
  156.4 0.0 all-gather.2.cloned.1.call-update
  156.4 60.8 %all-gather.2.cloned.1.call-done = bf16[5120,1024]{1,0:T(8,128)(2,1)} async-done(((bf16[640,1024]{1,0:T(8,128)(2,1)}), bf16[5120,1024]{1,0:T(8,128)(2,1)}) %all-gather.2.cloned.1.call-update) | async-done | bytes 10485776 | tf_op jit(solution)/shard_map/all_gather | solution.py:85
  217.2 7.2 %convolution_convert_fusion = bf16[1024,320]{0,1:T(8,128)(2,1)} fusion(bf16[5120,320]{0,1:T(8,128)(2,1)S(1)} %copy-done, bf16[5120,1024]{1,0:T(8,128)(2,1)} %all-gather.2.cloned.1.call-done), kind=kOutput, calls=%fused_computation.23 | convolution fusion | flops 3355770880 | bytes 14417920 | tf_op jit(solution)/shard_map/kt,kd->td/dot_general | solution.py:83
  (53 shorter events, 0.3 us)
Async XLA Ops:
  6.5 210.6 %copy-start = (bf16[5120,320]{0,1:T(8,128)(2,1)S(1)}, bf16[5120,320]{0,1:T(8,128)(2,1)}, u32[]{:S(2)}) copy-start(bf16[5120,320]{0,1:T(8,128)(2,1)} %param.15) | copy-start | bytes 9830404
  6.5 210.6 %all-gather.2.cloned.1.call-start = ((), (), s32[]{:S(2)}) async-start(), calls=%async_computation | async-start | bytes 11796480 | tf_op jit(solution)/shard_map/all_gather | solution.py:85
  7.6 16.6 %copy-start.8 = (f32[10,4,256]{2,1,0:T(4,128)}, f32[10,4,256]{2,1,0:T(4,128)S(1)}, u32[]{:S(2)}) copy-start(f32[10,4,256]{2,1,0:T(4,128)S(1)} %mul.141) | copy-start | bytes 122884
  8.6 0.6 copy-start.5
  12.0 12.1 %copy-start.6 = (f32[10,4,256]{2,1,0:T(4,128)}, f32[10,4,256]{2,1,0:T(4,128)S(1)}, u32[]{:S(2)}) copy-start(f32[10,4,256]{2,1,0:T(4,128)S(1)} %reduce_window_sum.42) | copy-start | bytes 122884
  39.9 59.4 %copy-start.3 = (bf16[1024,128]{1,0:T(8,128)(2,1)S(1)}, bf16[1024,128]{1,0:T(8,128)(2,1)}, u32[]{:S(2)}) copy-start(bf16[1024,128]{1,0:T(8,128)(2,1)} %param.13) | copy-start | bytes 786436
  41.9 11.0 %collective-permute-start.5 = (f32[10,128,64]{1,2,0:T(8,128)}, f32[10,128,64]{1,2,0:T(8,128)}, u32[]{:S(2)}, u32[]{:S(2)}) collective-permute-start(f32[10,128,64]{1,2,0:T(8,128)} %copy.39), channel_id=1, source_target_pairs={{0,8},{8,16},{16,24},{24,32},{32,40},{40,48},{48,56},{56,64},{64,7... | collective-permute-start | bytes 983048 | tf_op jit(solution)/shard_map/ppermute | solution.py:15
  53.0 9.9 %collective-permute-start.6 = (f32[10,128,64]{1,2,0:T(8,128)}, f32[10,128,64]{1,2,0:T(8,128)}, u32[]{:S(2)}, u32[]{:S(2)}) collective-permute-start(f32[10,128,64]{1,2,0:T(8,128)} %collective-permute-done.5), channel_id=1, source_target_pairs={{0,8},{8,16},{16,24},{24,32},{32,40},{40,48},{48,56},{56,64},{64,7... | collective-permute-start | bytes 983048 | tf_op jit(solution)/shard_map/ppermute | solution.py:15
  57.8 5.0 %collective-permute-start = (f32[10]{0:T(128)S(1)}, f32[10]{0:T(128)S(1)}, u32[]{:S(2)}, u32[]{:S(2)}) collective-permute-start(f32[10]{0:T(128)S(1)} %negate_exponential_fusion), channel_id=1, source_target_pairs={{0,8},{8,16},{16,24},{24,32},{32,40},{40,48},{48,56},{56,64},{64,7... | collective-permute-start | bytes 128 | tf_op jit(solution)/shard_map/ppermute | solution.py:15
  64.8 12.3 %collective-permute-start.7 = (f32[10,128,64]{1,2,0:T(8,128)}, f32[10,128,64]{1,2,0:T(8,128)}, u32[]{:S(2)}, u32[]{:S(2)}) collective-permute-start(f32[10,128,64]{1,2,0:T(8,128)} %add_select_fusion.4), channel_id=1, source_target_pairs={{0,16},{8,24},{16,32},{24,40},{32,48},{40,56},{48,64},{56,72},{64,... | collective-permute-start | bytes 983048 | tf_op jit(solution)/shard_map/ppermute | solution.py:15
  71.3 5.7 %collective-permute-start.1 = (f32[10]{0:T(128)S(1)}, f32[10]{0:T(128)S(1)}, u32[]{:S(2)}, u32[]{:S(2)}) collective-permute-start(f32[10]{0:T(128)S(1)} %broadcast_select_fusion.1), channel_id=1, source_target_pairs={{0,8},{8,16},{16,24},{24,32},{32,40},{40,48},{48,56},{56,64},{64,7... | collective-permute-start | bytes 128 | tf_op jit(solution)/shard_map/ppermute | solution.py:15
  77.0 22.3 %copy-start.12 = (f32[10]{0:T(128)}, f32[10]{0:T(128)S(1)}, u32[]{:S(2)}) copy-start(f32[10]{0:T(128)S(1)} %broadcast_select_fusion) | copy-start | bytes 124
  79.0 34.9 %collective-permute-start.8 = (f32[10,128,64]{1,2,0:T(8,128)}, f32[10,128,64]{1,2,0:T(8,128)}, u32[]{:S(2)}, u32[]{:S(2)}) collective-permute-start(f32[10,128,64]{1,2,0:T(8,128)} %add_select_fusion.3), channel_id=1, source_target_pairs={{0,32},{8,40},{16,48},{24,56},{32,64},{40,72},{48,80},{56,88},{64,... | collective-permute-start | bytes 983048 | tf_op jit(solution)/shard_map/ppermute | solution.py:15
  101.5 44.0 %copy-start.4 = (bf16[1024,128]{1,0:T(8,128)(2,1)S(1)}, bf16[1024,128]{1,0:T(8,128)(2,1)}, u32[]{:S(2)}) copy-start(bf16[1024,128]{1,0:T(8,128)(2,1)} %param.14) | copy-start | bytes 786436
  104.7 8.5 %collective-permute-start.2 = (f32[10]{0:T(128)}, f32[10]{0:T(128)S(1)}, u32[]{:S(2)}, u32[]{:S(2)}) collective-permute-start(f32[10]{0:T(128)} %copy-done.12), channel_id=1, source_target_pairs={{0,16},{8,24},{16,32},{24,40},{32,48},{40,56},{48,64},{56,72},{64,... | collective-permute-start | bytes 128 | tf_op jit(solution)/shard_map/ppermute | solution.py:15
  113.8 1.9 copy-start.13
  115.7 11.8 %collective-permute-start.9 = (f32[10,128,64]{1,2,0:T(8,128)}, f32[10,128,64]{1,2,0:T(8,128)}, u32[]{:S(2)}, u32[]{:S(2)}) collective-permute-start(f32[10,128,64]{1,2,0:T(8,128)} %add_select_fusion.2), channel_id=1, source_target_pairs={{0,64},{8,72},{16,80},{24,88},{32,96},{40,104},{48,112},{56,120},{... | collective-permute-start | bytes 983048 | tf_op jit(solution)/shard_map/ppermute | solution.py:15
  122.1 4.7 %collective-permute-start.3 = (f32[10]{0:T(128)}, f32[10]{0:T(128)S(1)}, u32[]{:S(2)}, u32[]{:S(2)}) collective-permute-start(f32[10]{0:T(128)} %copy-done.13), channel_id=1, source_target_pairs={{0,32},{8,40},{16,48},{24,56},{32,64},{40,72},{48,80},{56,88},{64,... | collective-permute-start | bytes 128 | tf_op jit(solution)/shard_map/ppermute | solution.py:15
  128.7 13.9 %collective-permute-start.10 = (f32[10,128,64]{1,2,0:T(8,128)S(1)}, f32[10,128,64]{1,2,0:T(8,128)S(1)}, u32[]{:S(2)}, u32[]{:S(2)}) collective-permute-start(f32[10,128,64]{1,2,0:T(8,128)S(1)} %add_select_fusion.1), channel_id=1, source_target_pairs={{0,128},{8,136},{16,144},{24,152},{32,160},{40,168},{48,176},{56,1... | collective-permute-start | bytes 983048 | tf_op jit(solution)/shard_map/ppermute | solution.py:15
  138.0 4.6 %collective-permute-start.4 = (f32[10]{0:T(128)S(1)}, f32[10]{0:T(128)S(1)}, u32[]{:S(2)}, u32[]{:S(2)}) collective-permute-start(f32[10]{0:T(128)S(1)} %broadcast_select_fusion.3), channel_id=1, source_target_pairs={{0,64},{8,72},{16,80},{24,88},{32,96},{40,104},{48,112},{56,120},{... | collective-permute-start | bytes 128 | tf_op jit(solution)/shard_map/ppermute | solution.py:15
  145.5 4.4 %copy-start.1 = (bf16[10,64,4,256]{3,2,1,0:T(4,128)(2,1)S(1)}, bf16[10,64,4,256]{3,2,1,0:T(4,128)(2,1)}, u32[]{:S(2)}) copy-start(bf16[10,64,4,256]{3,2,1,0:T(4,128)(2,1)} %reshape.94) | copy-start | bytes 3932164
  145.5 4.4 %copy-start.2 = (f32[4,256,256]{2,1,0:T(8,128)S(1)}, f32[4,256,256]{2,1,0:T(8,128)}, u32[]{:S(2)}) copy-start(f32[4,256,256]{2,1,0:T(8,128)} %fusion.22) | copy-start | bytes 3145732
  145.5 4.5 %copy-start.7 = (f32[10,4,256]{2,1,0:T(4,128)S(1)}, f32[10,4,256]{2,1,0:T(4,128)}, u32[]{:S(2)}) copy-start(f32[10,4,256]{2,1,0:T(4,128)} %copy-done.6) | copy-start | bytes 122884
  145.5 4.5 %copy-start.9 = (f32[10,4,256]{2,1,0:T(4,128)S(1)}, f32[10,4,256]{2,1,0:T(4,128)}, u32[]{:S(2)}) copy-start(f32[10,4,256]{2,1,0:T(4,128)} %copy-done.8) | copy-start | bytes 122884
  145.5 4.5 %copy-start.10 = (pred[256,256]{1,0:T(8,128)(4,1)S(1)}, pred[256,256]{1,0:T(8,128)(4,1)}, u32[]{:S(2)}) copy-start(pred[256,256]{1,0:T(8,128)(4,1)} %iota_compare_fusion) | copy-start | bytes 196612
  145.5 4.5 %copy-start.11 = (f32[10,4,256]{2,1,0:T(4,128)S(1)}, f32[10,4,256]{2,1,0:T(4,128)}, u32[]{:S(2)}) copy-start(f32[10,4,256]{2,1,0:T(4,128)} %get-tuple-element.80) | copy-start | bytes 122884
  145.5 4.5 %copy-start.14 = (f32[10]{0:T(128)S(1)}, f32[10]{0:T(128)}, u32[]{:S(2)}) copy-start(f32[10]{0:T(128)} %param.12) | copy-start | bytes 124
Sparse Core Ops, SparseCore 0:
  156.5 60.5 all-gather.1
where the time goes:
time: 232 us; the launch traced here: 231 us
  waiting for transfers between devices  81 us (35%)
  starting transfers between devices  65.2 us (28%)
  other arithmetic  33.6 us (14%)
  matrix products  23.4 us (10%)
  local copies, waits for them, and re-layouts  14.2 us (6%)
  between operations  13.7 us (6%)
    ppermute x11, starting transfers between devices, shifted(): return lax.ppermute(value, 'seq', [(i, i + d) for i in range(peers - d)])  65.2 us
    all_gather x1, waiting for transfers between devices, on_device(): lax.all_gather(mixed_columns, 'grp', axis=0, tiled=True)  60.8 us
    ppermute x11, waiting for transfers between devices, shifted(): return lax.ppermute(value, 'seq', [(i, i + d) for i in range(peers - d)])  20.2 us
    add x4, other arithmetic, advance(): return (decay[:, None, None] * state + digest_record, state)  8.81 us
    select_n x5, other arithmetic, carry_in(): state = jnp.where(reached, decay[:, None, None] * state_r + state, state)  7.74 us
    dot_general x1, matrix products, on_device(): jnp.einsum('kt,kd->td', lax.all_gather(mixed_columns, 'grp', axis=0, tile...  7.17 us
    dynamic_update_slice x4, other arithmetic, on_device(): lax.scan(advance, zero_state, (block_decay.T, summaries))  6.89 us
    dot_general x1, matrix products, on_device(): jnp.einsum('hcjn,hpcj->chnp', weighted_terms, channels, preferred_element...  5.63 us
  transfers between devices with their start and end apart: 12, of which 7 were waited for; matrix products, arithmetic and copies ran while one was open for 4% of the time, Pallas kernels for 0%

commit v1 on v0

--- a/solution.py
+++ b/solution.py
@@ -82,7 +82,9 @@
     mixed_columns = mixed.astype(jnp.bfloat16).reshape(heads_here * HP, tokens_here)
     result = jnp.einsum(
         "kt,kd->td",
-        lax.all_gather(mixed_columns, "grp", axis=0, tiled=True),
+        jnp.concatenate(
+            lax.all_to_all(jnp.stack([mixed_columns] * lax.axis_size("grp")), "grp", 0, 0), axis=0
+        ),
         out_weight,
         preferred_element_type=jnp.float32,
     )

time: 232 us -> 285 us (1.23)
  blocking collectives: 0 us -> 125 us
  waiting for transfers between devices: 81 us -> 20.3 us
  between operations: 13.7 us -> 0.29 us
  local copies, waits for them, and re-layouts: 14.2 us -> 18.4 us
    all_to_all x0 -> x1, blocking collectives: none -> 125 us  [on_device(): lax.all_to_all(jnp.stack([mixed_columns] * lax.axis_size('grp')), 'grp',...]
    all_gather x1 -> x0, waiting for transfers between devices: 60.8 us -> none  [on_device(): lax.all_gather(mixed_columns, 'grp', axis=0, tiled=True)]
    another operation x3 -> x4, local copies, waits for them, and re-layouts: 0.08 us -> 5.4 us  [the longest x1 5.33 us: on_device(): jnp.stack([mixed_columns] * lax.axis_size('grp'))]
  transfers between devices with their start and end apart: 12 -> 11, of which waited for: 7 -> 6; matrix products, arithmetic and copies ran while one was open for 4% -> 3% of each run, Pallas kernels for 0% -> 0%
where the time goes in v1:
time: 285 us; the launch traced here: 283 us
  blocking collectives  125 us (44%)
  starting transfers between devices  65.3 us (23%)
  other arithmetic  33.5 us (12%)
  matrix products  20.7 us (7%)
  waiting for transfers between devices  20.3 us (7%)
  local copies, waits for them, and re-layouts  18.4 us (6%)
    all_to_all x1, blocking collectives, on_device(): lax.all_to_all(jnp.stack([mixed_columns] * lax.axis_size('grp')), 'grp',...  125 us
    ppermute x11, starting transfers between devices, shifted(): return lax.ppermute(value, 'seq', [(i, i + d) for i in range(peers - d)])  65.3 us
    ppermute x11, waiting for transfers between devices, shifted(): return lax.ppermute(value, 'seq', [(i, i + d) for i in range(peers - d)])  20.3 us
    add x4, other arithmetic, advance(): return (decay[:, None, None] * state + digest_record, state)  8.81 us
    select_n x5, other arithmetic, carry_in(): state = jnp.where(reached, decay[:, None, None] * state_r + state, state)  7.74 us
    dynamic_update_slice x4, other arithmetic, on_device(): lax.scan(advance, zero_state, (block_decay.T, summaries))  6.86 us
  transfers between devices with their start and end apart: 11, of which 6 were waited for; matrix products, arithmetic and copies ran while one was open for 3% of the time, Pallas kernels for 0%

profile of v1, /device:TPU:1, one launch (start us, length us, event | category | flops | bytes accessed | tf_op | source)
XLA Modules:
  0.0 283.3 jit_solution(9524548111312250898)
XLA Ops:
  0.0 1.0 mul.141
  1.0 1.0 fusion.19
  2.1 0.6 copy-done.5
  2.8 2.3 reduce-window.6
  5.1 0.2 slice_reduce_fusion
  5.3 0.1 broadcast_add_fusion
  5.5 0.1 slice.15
  5.5 0.1 copy.33
  5.6 0.1 copy.34
  5.7 0.6 fusion.20
  6.4 1.8 convert_element_type.24
  8.2 3.8 %reshape.96 = bf16[10,64,4,256]{3,2,1,0:T(4,128)(2,1)} reshape(bf16[640,1024]{1,0:T(8,128)(2,1)} %param.9) | data formatting | bytes 2621440 | tf_op jit(solution)/shard_map/reshape | solution.py:36
  12.0 5.6 %fusion.8 = f32[4,10,128,64]{3,2,1,0:T(8,128)} fusion(f32[10,4,256]{2,0,1:T(8,128)S(1)} %copy.35, f32[4,256,128]{2,1,0:T(8,128)} %convert_element_type.24, bf16[10,64,4,256]{3,2,1,0:T(4,128)(2,1)} %reshape.96), kind=kOutput, calls=%fused_computation.13 | convolution fusion | flops 170393600 | bytes 3186688 | tf_op jit(solution)/shard_map/hcjn,hpcj->chnp/dot_general | solution.py:59
  17.6 15.7 %while.13 = (s32[]{:T(128)}, f32[10,128,64]{2,1,0:T(8,128)}, f32[4,10,128,64]{3,2,1,0:T(8,128)}, f32[4,10]{1,0:T(4,128)S(1)}, f32[4,10,128,64]{3,2,1,0:T(8,128)}, /*index=5*/s32[]{:T(128)}, s32[]{:T(128)}) while((s32[]{:T(128)}, f32[10,128,64]{2,1,0:T(8,128)}, f32[4,10,128,64]{3,2,1,0:T(8,128)}, f32[4,10]{1,0:T(4,128)S(1)}, ...), condition=%wide.region_3.4_spmd.clone, body=%wide.region_2.3_spmd.clone.sunk | while | flops 327683 | bytes 2293988 | solution.py:69
  17.6 0.9 bitcast_dynamic-update-slice_fusion.2
  18.5 2.1 bitcast_add_fusion.2
  20.6 2.0 bitcast_dynamic-update-slice_fusion.2
  22.5 2.3 bitcast_add_fusion.2
  24.8 2.0 bitcast_dynamic-update-slice_fusion.2
  26.8 2.3 bitcast_add_fusion.2
  29.0 2.0 bitcast_dynamic-update-slice_fusion.2
  31.0 2.3 bitcast_add_fusion.2
  33.3 2.1 copy.39
  35.4 5.1 %collective-permute-start.5 = (f32[10,128,64]{1,2,0:T(8,128)}, f32[10,128,64]{1,2,0:T(8,128)}, u32[]{:S(2)}, u32[]{:S(2)}) collective-permute-start(f32[10,128,64]{1,2,0:T(8,128)} %copy.39), channel_id=1, source_target_pairs={{0,8},{8,16},{16,24},{24,32},{32,40},{40,48},{48,56},{56,64},{64,7... | collective-permute-start | bytes 983048 | tf_op jit(solution)/shard_map/ppermute | solution.py:15
  40.5 6.0 %collective-permute-done.5 = f32[10,128,64]{1,2,0:T(8,128)} collective-permute-done((f32[10,128,64]{1,2,0:T(8,128)}, f32[10,128,64]{1,2,0:T(8,128)}, u32[]{:S(2)}, u32[]{:S(2)}) %collective-permute-start.5) | collective-permute-done | bytes 327712 | tf_op jit(solution)/shard_map/ppermute | solution.py:15
  46.4 4.8 %collective-permute-start.6 = (f32[10,128,64]{1,2,0:T(8,128)}, f32[10,128,64]{1,2,0:T(8,128)}, u32[]{:S(2)}, u32[]{:S(2)}) collective-permute-start(f32[10,128,64]{1,2,0:T(8,128)} %collective-permute-done.5), channel_id=1, source_target_pairs={{0,8},{8,16},{16,24},{24,32},{32,40},{40,48},{48,56},{56,64},{64,7... | collective-permute-start | bytes 983048 | tf_op jit(solution)/shard_map/ppermute | solution.py:15
  51.2 2.8 collective-permute-start
  54.1 2.2 collective-permute-done
  56.3 0.0 collective-permute-done.6
  56.3 1.9 add_select_fusion.4
  58.2 6.6 %collective-permute-start.7 = (f32[10,128,64]{1,2,0:T(8,128)}, f32[10,128,64]{1,2,0:T(8,128)}, u32[]{:S(2)}, u32[]{:S(2)}) collective-permute-start(f32[10,128,64]{1,2,0:T(8,128)} %add_select_fusion.4), channel_id=1, source_target_pairs={{0,16},{8,24},{16,32},{24,40},{32,48},{40,56},{48,64},{56,72},{64,... | collective-permute-start | bytes 983048 | tf_op jit(solution)/shard_map/ppermute | solution.py:15
  64.7 5.0 %collective-permute-start.1 = (f32[10]{0:T(128)S(1)}, f32[10]{0:T(128)S(1)}, u32[]{:S(2)}, u32[]{:S(2)}) collective-permute-start(f32[10]{0:T(128)S(1)} %broadcast_select_fusion.1), channel_id=1, source_target_pairs={{0,8},{8,16},{16,24},{24,32},{32,40},{40,48},{48,56},{56,64},{64,7... | collective-permute-start | bytes 128 | tf_op jit(solution)/shard_map/ppermute | solution.py:15
  69.7 0.7 collective-permute-done.1
  70.5 1.9 add_select_fusion.3
  72.4 20.3 %collective-permute-start.8 = (f32[10,128,64]{1,2,0:T(8,128)}, f32[10,128,64]{1,2,0:T(8,128)}, u32[]{:S(2)}, u32[]{:S(2)}) collective-permute-start(f32[10,128,64]{1,2,0:T(8,128)} %add_select_fusion.3), channel_id=1, source_target_pairs={{0,32},{8,40},{16,48},{24,56},{32,64},{40,72},{48,80},{56,88},{64,... | collective-permute-start | bytes 983048 | tf_op jit(solution)/shard_map/ppermute | solution.py:15
  92.7 2.2 fusion.22
  94.9 1.5 reshape.97
  96.5 0.9 reduce_sum.18
  97.3 0.7 reduce_window_sum.43
  98.1 1.3 collective-permute-start.2
  99.4 7.2 %collective-permute-done.2 = f32[10]{0:T(128)S(1)} collective-permute-done((f32[10]{0:T(128)}, f32[10]{0:T(128)S(1)}, u32[]{:S(2)}, u32[]{:S(2)}) %collective-permute-start.2) | collective-permute-done | bytes 72 | tf_op jit(solution)/shard_map/ppermute | solution.py:15
  106.6 0.6 broadcast_select_fusion.2
  107.2 1.9 add_select_fusion.2
  109.1 5.6 %collective-permute-start.9 = (f32[10,128,64]{1,2,0:T(8,128)}, f32[10,128,64]{1,2,0:T(8,128)}, u32[]{:S(2)}, u32[]{:S(2)}) collective-permute-start(f32[10,128,64]{1,2,0:T(8,128)} %add_select_fusion.2), channel_id=1, source_target_pairs={{0,64},{8,72},{16,80},{24,88},{32,96},{40,104},{48,112},{56,120},{... | collective-permute-start | bytes 983048 | tf_op jit(solution)/shard_map/ppermute | solution.py:15
  114.7 0.7 exponential_bitcast_fusion
  115.4 0.1 copy.38
  115.5 3.8 %collective-permute-start.3 = (f32[10]{0:T(128)}, f32[10]{0:T(128)S(1)}, u32[]{:S(2)}, u32[]{:S(2)}) collective-permute-start(f32[10]{0:T(128)} %copy-done.13), channel_id=1, source_target_pairs={{0,32},{8,40},{16,48},{24,56},{32,64},{40,72},{48,80},{56,88},{64,... | collective-permute-start | bytes 128 | tf_op jit(solution)/shard_map/ppermute | solution.py:15
  119.3 0.9 collective-permute-done.3
  120.2 0.7 broadcast_select_fusion.3
  120.9 1.2 add_select_fusion.1
  122.1 8.7 %collective-permute-start.10 = (f32[10,128,64]{1,2,0:T(8,128)S(1)}, f32[10,128,64]{1,2,0:T(8,128)S(1)}, u32[]{:S(2)}, u32[]{:S(2)}) collective-permute-start(f32[10,128,64]{1,2,0:T(8,128)S(1)} %add_select_fusion.1), channel_id=1, source_target_pairs={{0,128},{8,136},{16,144},{24,152},{32,160},{40,168},{48,176},{56,1... | collective-permute-start | bytes 983048 | tf_op jit(solution)/shard_map/ppermute | solution.py:15
  130.8 0.6 iota_compare_fusion
  131.4 1.3 collective-permute-start.4
  132.7 3.3 %collective-permute-done.4 = f32[10]{0:T(128)S(1)} collective-permute-done((f32[10]{0:T(128)S(1)}, f32[10]{0:T(128)S(1)}, u32[]{:S(2)}, u32[]{:S(2)}) %collective-permute-start.4) | collective-permute-done | bytes 72 | tf_op jit(solution)/shard_map/ppermute | solution.py:15
  136.0 0.8 add_select_fusion
  136.9 2.0 copy.40
  138.9 0.0 copy-start.14
  139.0 4.4 %fusion.12 = f32[4,10,64,256]{3,2,0,1:T(8,128)S(1)} fusion(bf16[4,256,128,1]{2,1,0,3:T(8,128)(2,1)S(1)} %bitcast.48, f32[4,10,128,64]{3,2,1,0:T(8,128)} %get-tuple-element.33, f32[10,128,64]{2,1,0:T(8,128)} %copy.40, f32[4,10]{1,0:T(4,128)S(1)} %copy.38), kind=kOutput, calls=%fused_computation.18 | convolution fusion | flops 1007288320 | bytes 4522144 | tf_op jit(solution)/shard_map/cin,chnp->hpci/dot_general | solution.py:78
  143.4 4.0 %fusion.11 = bf16[10,64,4,256]{3,1,2,0:T(8,128)(2,1)S(1)} fusion(f32[4,10,64,256]{3,2,0,1:T(8,128)S(1)} %fusion.12, f32[10,4,256]{2,1,0:T(4,128)S(1)} %copy-done.9, f32[10,4,256]{2,1,0:T(4,128)S(1)} %copy-done.7, f32[4,256,256]{2,1,0:T(8,128)S(1)} %copy-done.2, pred[256,256]{1,0:T(8,128)(4,1)S(1)} %copy-done.10, bf16[10,64,4,256]{3,2,1,0:T(4,128)(2,1)S(1)} %copy-done.1, ...), kind=kOutput, calls=%fused_computation.17 | convolution fusion | flops 355205120 | bytes 6479912 | tf_op jit(solution)/shard_map/hcij,hpcj->hpci/dot_general | solution.py:54
  147.4 1.0 copy.43
  148.4 0.3 copy.47
  148.7 5.3 %stack.3 = bf16[8,640,1024]{2,1,0:T(8,128)(2,1)} broadcast(bf16[640,1024]{1,0:T(8,128)(2,1)S(1)} %bitcast.44), dimensions={1,2} | broadcast | bytes 11796480 | tf_op jit(solution)/shard_map/stack | solution.py:86
  154.0 124.7 %all_to_all.5 = bf16[8,640,1024]{2,1,0:T(8,128)(2,1)S(1)} all-to-all(bf16[8,640,1024]{2,1,0:T(8,128)(2,1)} %stack.3), channel_id=1, replica_groups=mesh['seq'=32,'grp'=8] {'grp'}, dimensions={0} | all-to-all | bytes 20971520 | tf_op jit(solution)/shard_map/all_to_all | solution.py:86
  278.8 4.5 %convolution_convert_fusion = bf16[1024,320]{0,1:T(8,128)(2,1)} fusion(bf16[5120,320]{0,1:T(8,128)(2,1)S(1)} %copy-done, bf16[5120,1024]{1,0:T(8,128)(2,1)S(1)} %bitcast.42), kind=kOutput, calls=%fused_computation.23 | convolution fusion | flops 3355770880 | bytes 14417920 | tf_op jit(solution)/shard_map/kt,kd->td/dot_general | solution.py:83
  (52 shorter events, 0.3 us)
Async XLA Ops:
  0.0 278.8 %copy-start = (bf16[5120,320]{0,1:T(8,128)(2,1)S(1)}, bf16[5120,320]{0,1:T(8,128)(2,1)}, u32[]{:S(2)}) copy-start(bf16[5120,320]{0,1:T(8,128)(2,1)} %param.15) | copy-start | bytes 9830404
  1.0 16.6 %copy-start.8 = (f32[10,4,256]{2,1,0:T(4,128)}, f32[10,4,256]{2,1,0:T(4,128)S(1)}, u32[]{:S(2)}) copy-start(f32[10,4,256]{2,1,0:T(4,128)S(1)} %mul.141) | copy-start | bytes 122884
  2.1 0.6 copy-start.5
  5.4 12.1 %copy-start.6 = (f32[10,4,256]{2,1,0:T(4,128)}, f32[10,4,256]{2,1,0:T(4,128)S(1)}, u32[]{:S(2)}) copy-start(f32[10,4,256]{2,1,0:T(4,128)S(1)} %reduce_window_sum.42) | copy-start | bytes 122884
  33.3 59.4 %copy-start.3 = (bf16[1024,128]{1,0:T(8,128)(2,1)S(1)}, bf16[1024,128]{1,0:T(8,128)(2,1)}, u32[]{:S(2)}) copy-start(bf16[1024,128]{1,0:T(8,128)(2,1)} %param.13) | copy-start | bytes 786436
  35.4 11.0 %collective-permute-start.5 = (f32[10,128,64]{1,2,0:T(8,128)}, f32[10,128,64]{1,2,0:T(8,128)}, u32[]{:S(2)}, u32[]{:S(2)}) collective-permute-start(f32[10,128,64]{1,2,0:T(8,128)} %copy.39), channel_id=1, source_target_pairs={{0,8},{8,16},{16,24},{24,32},{32,40},{40,48},{48,56},{56,64},{64,7... | collective-permute-start | bytes 983048 | tf_op jit(solution)/shard_map/ppermute | solution.py:15
  46.4 9.9 %collective-permute-start.6 = (f32[10,128,64]{1,2,0:T(8,128)}, f32[10,128,64]{1,2,0:T(8,128)}, u32[]{:S(2)}, u32[]{:S(2)}) collective-permute-start(f32[10,128,64]{1,2,0:T(8,128)} %collective-permute-done.5), channel_id=1, source_target_pairs={{0,8},{8,16},{16,24},{24,32},{32,40},{40,48},{48,56},{56,64},{64,7... | collective-permute-start | bytes 983048 | tf_op jit(solution)/shard_map/ppermute | solution.py:15
  51.2 5.0 %collective-permute-start = (f32[10]{0:T(128)S(1)}, f32[10]{0:T(128)S(1)}, u32[]{:S(2)}, u32[]{:S(2)}) collective-permute-start(f32[10]{0:T(128)S(1)} %negate_exponential_fusion), channel_id=1, source_target_pairs={{0,8},{8,16},{16,24},{24,32},{32,40},{40,48},{48,56},{56,64},{64,7... | collective-permute-start | bytes 128 | tf_op jit(solution)/shard_map/ppermute | solution.py:15
  58.2 12.3 %collective-permute-start.7 = (f32[10,128,64]{1,2,0:T(8,128)}, f32[10,128,64]{1,2,0:T(8,128)}, u32[]{:S(2)}, u32[]{:S(2)}) collective-permute-start(f32[10,128,64]{1,2,0:T(8,128)} %add_select_fusion.4), channel_id=1, source_target_pairs={{0,16},{8,24},{16,32},{24,40},{32,48},{40,56},{48,64},{56,72},{64,... | collective-permute-start | bytes 983048 | tf_op jit(solution)/shard_map/ppermute | solution.py:15
  64.7 5.7 %collective-permute-start.1 = (f32[10]{0:T(128)S(1)}, f32[10]{0:T(128)S(1)}, u32[]{:S(2)}, u32[]{:S(2)}) collective-permute-start(f32[10]{0:T(128)S(1)} %broadcast_select_fusion.1), channel_id=1, source_target_pairs={{0,8},{8,16},{16,24},{24,32},{32,40},{40,48},{48,56},{56,64},{64,7... | collective-permute-start | bytes 128 | tf_op jit(solution)/shard_map/ppermute | solution.py:15
  70.5 22.3 %copy-start.12 = (f32[10]{0:T(128)}, f32[10]{0:T(128)S(1)}, u32[]{:S(2)}) copy-start(f32[10]{0:T(128)S(1)} %broadcast_select_fusion) | copy-start | bytes 124
  72.4 34.8 %collective-permute-start.8 = (f32[10,128,64]{1,2,0:T(8,128)}, f32[10,128,64]{1,2,0:T(8,128)}, u32[]{:S(2)}, u32[]{:S(2)}) collective-permute-start(f32[10,128,64]{1,2,0:T(8,128)} %add_select_fusion.3), channel_id=1, source_target_pairs={{0,32},{8,40},{16,48},{24,56},{32,64},{40,72},{48,80},{56,88},{64,... | collective-permute-start | bytes 983048 | tf_op jit(solution)/shard_map/ppermute | solution.py:15
  94.9 44.0 %copy-start.4 = (bf16[1024,128]{1,0:T(8,128)(2,1)S(1)}, bf16[1024,128]{1,0:T(8,128)(2,1)}, u32[]{:S(2)}) copy-start(bf16[1024,128]{1,0:T(8,128)(2,1)} %param.14) | copy-start | bytes 786436
  98.1 8.5 %collective-permute-start.2 = (f32[10]{0:T(128)}, f32[10]{0:T(128)S(1)}, u32[]{:S(2)}, u32[]{:S(2)}) collective-permute-start(f32[10]{0:T(128)} %copy-done.12), channel_id=1, source_target_pairs={{0,16},{8,24},{16,32},{24,40},{32,48},{40,56},{48,64},{56,72},{64,... | collective-permute-start | bytes 128 | tf_op jit(solution)/shard_map/ppermute | solution.py:15
  107.2 1.9 copy-start.13
  109.1 11.8 %collective-permute-start.9 = (f32[10,128,64]{1,2,0:T(8,128)}, f32[10,128,64]{1,2,0:T(8,128)}, u32[]{:S(2)}, u32[]{:S(2)}) collective-permute-start(f32[10,128,64]{1,2,0:T(8,128)} %add_select_fusion.2), channel_id=1, source_target_pairs={{0,64},{8,72},{16,80},{24,88},{32,96},{40,104},{48,112},{56,120},{... | collective-permute-start | bytes 983048 | tf_op jit(solution)/shard_map/ppermute | solution.py:15
  115.5 4.7 %collective-permute-start.3 = (f32[10]{0:T(128)}, f32[10]{0:T(128)S(1)}, u32[]{:S(2)}, u32[]{:S(2)}) collective-permute-start(f32[10]{0:T(128)} %copy-done.13), channel_id=1, source_target_pairs={{0,32},{8,40},{16,48},{24,56},{32,64},{40,72},{48,80},{56,88},{64,... | collective-permute-start | bytes 128 | tf_op jit(solution)/shard_map/ppermute | solution.py:15
  122.1 13.9 %collective-permute-start.10 = (f32[10,128,64]{1,2,0:T(8,128)S(1)}, f32[10,128,64]{1,2,0:T(8,128)S(1)}, u32[]{:S(2)}, u32[]{:S(2)}) collective-permute-start(f32[10,128,64]{1,2,0:T(8,128)S(1)} %add_select_fusion.1), channel_id=1, source_target_pairs={{0,128},{8,136},{16,144},{24,152},{32,160},{40,168},{48,176},{56,1... | collective-permute-start | bytes 983048 | tf_op jit(solution)/shard_map/ppermute | solution.py:15
  131.4 4.6 %collective-permute-start.4 = (f32[10]{0:T(128)S(1)}, f32[10]{0:T(128)S(1)}, u32[]{:S(2)}, u32[]{:S(2)}) collective-permute-start(f32[10]{0:T(128)S(1)} %broadcast_select_fusion.3), channel_id=1, source_target_pairs={{0,64},{8,72},{16,80},{24,88},{32,96},{40,104},{48,112},{56,120},{... | collective-permute-start | bytes 128 | tf_op jit(solution)/shard_map/ppermute | solution.py:15
  138.9 4.4 %copy-start.1 = (bf16[10,64,4,256]{3,2,1,0:T(4,128)(2,1)S(1)}, bf16[10,64,4,256]{3,2,1,0:T(4,128)(2,1)}, u32[]{:S(2)}) copy-start(bf16[10,64,4,256]{3,2,1,0:T(4,128)(2,1)} %reshape.96) | copy-start | bytes 3932164
  138.9 4.4 %copy-start.2 = (f32[4,256,256]{2,1,0:T(8,128)S(1)}, f32[4,256,256]{2,1,0:T(8,128)}, u32[]{:S(2)}) copy-start(f32[4,256,256]{2,1,0:T(8,128)} %fusion.22) | copy-start | bytes 3145732
  138.9 4.5 %copy-start.7 = (f32[10,4,256]{2,1,0:T(4,128)S(1)}, f32[10,4,256]{2,1,0:T(4,128)}, u32[]{:S(2)}) copy-start(f32[10,4,256]{2,1,0:T(4,128)} %copy-done.6) | copy-start | bytes 122884
  138.9 4.5 %copy-start.9 = (f32[10,4,256]{2,1,0:T(4,128)S(1)}, f32[10,4,256]{2,1,0:T(4,128)}, u32[]{:S(2)}) copy-start(f32[10,4,256]{2,1,0:T(4,128)} %copy-done.8) | copy-start | bytes 122884
  138.9 4.5 %copy-start.10 = (pred[256,256]{1,0:T(8,128)(4,1)S(1)}, pred[256,256]{1,0:T(8,128)(4,1)}, u32[]{:S(2)}) copy-start(pred[256,256]{1,0:T(8,128)(4,1)} %iota_compare_fusion) | copy-start | bytes 196612
  138.9 4.5 %copy-start.11 = (f32[10,4,256]{2,1,0:T(4,128)S(1)}, f32[10,4,256]{2,1,0:T(4,128)}, u32[]{:S(2)}) copy-start(f32[10,4,256]{2,1,0:T(4,128)} %get-tuple-element.80) | copy-start | bytes 122884
  138.9 4.5 %copy-start.14 = (f32[10]{0:T(128)S(1)}, f32[10]{0:T(128)}, u32[]{:S(2)}) copy-start(f32[10]{0:T(128)} %param.12) | copy-start | bytes 124
